TPU v7x, 256 devices: a whole 4x4x8 slice. The times are simulated.
256 devices in a mesh: row: 8 (over y, core), col: 32 (over x, z).
Axes of the slice: x: 4, y: 4, z: 8, core: 2. Of those that a mesh axis runs over, the one named last changes fastest.
Arguments:
- stored: float32 [20, 8, 128, 5, 32, 128], P(None, 'row', None, None, 'col'), may hold values from -1 to 13
- rhs: float32 [5, 32, 128, 128], P(None, 'col'), may hold values from -60 to 60
Outputs:
- solution: float32 [5, 32, 128, 128], P(None, 'col')
- residual: float32 [5, 32, 128, 128], P(None, 'col')
All inputs are finite; a program needn't handle non-finite values.
Results may differ from a plain program's by a relative error of at most 0.0003.
Values sent between devices are 32-bit elements; how exact they have to be, the bound alone decides.
A program may use at most 128 MiB of HBM per device.

v0:
```python
import jax
import jax.numpy as jnp
from jax import lax
from jax.sharding import PartitionSpec as P

ITERS = 2
HIGHEST = lax.Precision.HIGHEST


def partner_2(value, axis, distance):
    mask = 2**distance
    pairs = [(source, source ^ mask) for source in range(lax.axis_size(axis))]
    return lax.ppermute(value, axis, pairs)


def spread(value, axis, source):
    kept = jnp.where(lax.axis_index(axis) == source, value, 0).astype(value.dtype)
    return lax.psum(kept, axis)


def gram_local(left_side, right_side):
    columns_n = left_side.shape[-1]
    return jnp.einsum(
        "nk,nl->kl",
        left_side.reshape(-1, columns_n),
        right_side.reshape(-1, columns_n),
        precision=HIGHEST,
        preferred_element_type=jnp.float32,
    )


def mix_right(vectors, matrix):
    columns_n = vectors.shape[-1]
    return jnp.dot(
        vectors.reshape(-1, columns_n),
        matrix,
        precision=HIGHEST,
        preferred_element_type=jnp.float32,
    ).reshape(vectors.shape)


def solve_spd(matrix, target):
    factor = jnp.linalg.cholesky(matrix)
    return jax.scipy.linalg.cho_solve((factor, True), target)


def to_rowset(column_set, row_index, col_index):
    low_bits = lax.axis_size("row").bit_length() - 1
    high_bits = lax.axis_size("col").bit_length() - 1
    current = column_set
    for bit_pos in range(low_bits):
        partner = partner_2(current, "col", bit_pos)
        differs = col_index >> bit_pos & 1 != row_index >> bit_pos & 1
        current = jnp.where(differs, partner, current)
    joined = current[:, None]
    for bit_pos in range(low_bits, high_bits):
        partner = partner_2(joined, "col", bit_pos)
        lower_half = col_index >> bit_pos & 1 == 0
        joined = jnp.where(
            lower_half,
            jnp.concatenate([joined, partner], axis=1),
            jnp.concatenate([partner, joined], axis=1),
        )
    return joined.reshape((-1,) + column_set.shape[1:])


def to_colset(row_set, col_index):
    rows_n = lax.axis_size("row")
    groups = lax.axis_size("col") // rows_n
    shape_in = row_set.shape
    regrouped = row_set.reshape(shape_in[:-3] + (shape_in[-3] // groups, groups) + shape_in[-2:])
    selected = lax.dynamic_index_in_dim(
        regrouped, col_index // rows_n, regrouped.ndim - 3, keepdims=False
    )
    return spread(selected, "row", col_index % rows_n)


def local_products(lower_part, column_set, row_set):
    columns_n = column_set.shape[-1]
    by_rows = jnp.dot(
        lower_part,
        column_set.reshape(-1, columns_n),
        precision=HIGHEST,
        preferred_element_type=jnp.float32,
    )
    by_columns = jnp.einsum(
        "nm,nk->mk",
        lower_part,
        row_set.reshape(-1, columns_n),
        precision=HIGHEST,
        preferred_element_type=jnp.float32,
    )
    return (by_rows, by_columns)


def columns_whole(by_columns, shape_out):
    return lax.psum(by_columns, "row").reshape(shape_out)


def rows_whole(by_rows, shape_out):
    return lax.psum(by_rows, "col").reshape(shape_out)


def per_device(stored, rhs):
    row_index = lax.axis_index("row")
    col_index = lax.axis_index("col")
    rows_n = lax.axis_size("row")
    cols_n = lax.axis_size("col")
    row_blocks = stored.shape[0]
    block_size = stored.shape[2]
    col_blocks = stored.shape[3]
    columns_n = rhs.shape[-1]
    block_rows = jnp.arange(row_blocks, dtype=jnp.int32) * rows_n + row_index
    block_cols = jnp.arange(col_blocks, dtype=jnp.int32) * cols_n + col_index
    weight = jnp.where(
        block_rows[:, None] > block_cols[None, :],
        1.0,
        jnp.where(block_rows[:, None] == block_cols[None, :], 0.5, 0.0),
    ).astype(jnp.float32)
    lower_part = (
        stored.reshape(row_blocks, block_size, col_blocks, block_size) * weight[:, None, :, None]
    ).reshape(row_blocks * block_size, col_blocks * block_size)
    start_set = rhs.reshape(col_blocks, block_size, columns_n)

    def reduce_grams(stacked):
        return lax.psum(stacked, "row")

    vectors = to_rowset(start_set, row_index, col_index)
    solution = jnp.zeros_like(vectors)
    residual = vectors
    direction = vectors
    gram_now = reduce_grams(gram_local(residual, residual)[None])[0]
    for iteration in range(ITERS):
        column_set = to_colset(direction, col_index)
        by_rows, by_columns = local_products(lower_part, column_set, direction)
        row_part = rows_whole(by_rows, direction.shape)
        applied = row_part + to_rowset(
            columns_whole(by_columns, column_set.shape), row_index, col_index
        )
        last_turn = iteration + 1 == ITERS
        gram_sums = reduce_grams(gram_local(direction, applied)[None])
        curvature = gram_sums[0]
        step_size = solve_spd(curvature, gram_now)
        solution = solution + mix_right(direction, step_size)
        residual = residual - mix_right(applied, step_size)
        if not last_turn:
            gram_next = reduce_grams(gram_local(residual, residual)[None])[0]
            mix_factor = solve_spd(gram_now, gram_next)
            direction = residual + mix_right(direction, mix_factor)
            gram_now = gram_next
    both_sets = to_colset(jnp.stack([solution, residual]), col_index)
    final_pair = (both_sets[0], both_sets[1])
    return (final_pair[0].reshape(rhs.shape), final_pair[1].reshape(rhs.shape))


def solution(mesh):
    placed = (P(None, "row", None, None, "col", None), P(None, "col", None, None))
    return jax.shard_map(
        per_device,
        mesh=mesh,
        in_specs=placed,
        out_specs=(P(None, "col", None, None), P(None, "col", None, None)),
        check_vma=False,
    )
```

profile of v0, /device:TPU:2, one launch (start us, length us, event | category | flops | bytes accessed | tf_op | source)
XLA Modules:
  0.0 995.7 jit_solution(8550308270842308896)
XLA Ops:
  9.2 7.9 collective-permute-done
  21.5 14.1 %collective-permute-done.1 = f32[5,128,128]{2,1,0:T(8,128)S(1)} collective-permute-done((f32[5,128,128]{2,1,0:T(8,128)S(1)}, f32[5,128,128]{2,1,0:T(8,128)S(1)}, u32[]{:S(2)}, u32[]{:S(2)}) %collective-permute-start.1) | collective-permute-done | bytes 327712 | tf_op jit(solution)/shard_map/ppermute | solution.py:13
  35.6 6.3 collective-permute-start.2
  41.9 14.5 %collective-permute-done.2 = f32[5,128,128]{2,1,0:T(8,128)S(1)} collective-permute-done((f32[5,128,128]{2,1,0:T(8,128)S(1)}, f32[5,128,128]{2,1,0:T(8,128)S(1)}, u32[]{:S(2)}, u32[]{:S(2)}) %collective-permute-start.2) | collective-permute-done | bytes 327712 | tf_op jit(solution)/shard_map/ppermute | solution.py:13
  57.1 6.7 collective-permute-done.3
  67.2 23.9 %multiply_reduce_fusion = f32[20,128,5,128]{3,2,1,0:T(8,128)} fusion(f32[20,1,128,5,1,128]{5,4,3,2,1,0:T(1,128)} %param.5, f32[20,5]{1,0:T(8,128)S(1)} %select_select_fusion.3), kind=kLoop, calls=%fused_computation.8 | loop fusion | flops 1638400 | bytes 13107600 | tf_op jit(solution)/shard_map/mul | solution.py:121
  91.9 14.6 %fusion.4 = f32[640,128]{1,0:T(8,128)} fusion(f32[2560,128]{1,0:T(8,128)S(1)} %bitcast.127, f32[320,8,5,128]{3,2,1,0:T(8,128)} %bitcast.123), kind=kOutput, calls=%fused_computation.4 | convolution fusion | flops 2516582400 | bytes 8192000 | tf_op jit(solution)/shard_map/nm,nk->mk/dot_general | solution.py:86
  106.6 65.4 %all-reduce.26.cloned.1.call-done = (f32[640,128]{1,0:T(8,128)}, f32[5,128,128]{2,1,0:T(8,128)}) async-done(((f32[640,128]{1,0:T(8,128)}, f32[5,128,128]{2,1,0:T(8,128)}), (f32[640,128]{1,0:T(8,128)}, f32[5,128,128]{2,1,0:T(8,128)})) %all-reduce.26.cloned.1.call-update) | async-done | bytes 655376 | tf_op jit(solution)/shard_map/psum | solution.py:18
  173.5 6.1 collective-permute-done.5
  183.5 10.9 %collective-permute-done.6 = f32[5,128,128]{2,1,0:T(8,128)S(1)} collective-permute-done((f32[5,128,128]{2,1,0:T(8,128)S(1)}, f32[5,128,128]{2,1,0:T(8,128)S(1)}, u32[]{:S(2)}, u32[]{:S(2)}) %collective-permute-start.6) | collective-permute-done | bytes 327712 | tf_op jit(solution)/shard_map/ppermute | solution.py:13
  200.2 10.1 %fusion.6 = f32[2560,128]{1,0:T(8,128)} fusion(f32[640,128]{1,0:T(8,128)S(1)} %copy-done.5, f32[320,8,5,128]{3,2,1,0:T(8,128)} %bitcast.124), kind=kOutput, calls=%fused_computation.6 | convolution fusion | flops 2516582400 | bytes 8192000 | tf_op jit(solution)/shard_map/dot_general | solution.py:80
  214.8 6.5 collective-permute-done.8
  228.5 11.5 %collective-permute-done.9 = f32[5,2,128,128]{3,2,0,1:T(8,128)S(1)} collective-permute-done((f32[5,2,128,128]{3,2,0,1:T(8,128)S(1)}, f32[5,2,128,128]{3,2,0,1:T(8,128)S(1)}, u32[]{:S(2)}, u32[]{:S(2)}) %collective-permute-start.9) | collective-permute-done | bytes 655392 | tf_op jit(solution)/shard_map/ppermute | solution.py:13
  241.3 126.0 %all-reduce.12.cloned.1.call-done = f32[2560,128]{1,0:T(8,128)} async-done(((f32[2560,128]{1,0:T(8,128)}), f32[2560,128]{1,0:T(8,128)}) %all-reduce.12.cloned.1.call-update) | async-done | bytes 1310736 | tf_op jit(solution)/shard_map/psum | solution.py:101
  372.4 62.7 %all-reduce.24.cloned.1.call-done = (f32[128,128]{0,1:T(8,128)}, f32[128,128]{0,1:T(8,128)}) async-done(((f32[128,128]{0,1:T(8,128)}, f32[128,128]{0,1:T(8,128)}), (f32[128,128]{0,1:T(8,128)}, f32[128,128]{0,1:T(8,128)})) %all-reduce.24.cloned.1.call-update) | async-done | bytes 131088 | tf_op jit(solution)/shard_map/psum | solution.py:126
  438.0 11.7 %cholesky.70 = f32[128,128]{1,0:T(8,128)S(1)} custom-call(f32[128,128]{1,0:T(8,128)S(1)} %get-tuple-element.12), custom_call_target="Cholesky" | custom-call | tf_op jit(solution)/shard_map/jit(cholesky)/cholesky | solution.py:43
  450.3 11.7 %cholesky.59 = f32[128,128]{1,0:T(8,128)S(1)} custom-call(f32[128,128]{1,0:T(8,128)S(1)} %get-tuple-element.13), custom_call_target="Cholesky" | custom-call | tf_op jit(solution)/shard_map/jit(cholesky)/cholesky | solution.py:43
  463.4 9.8 custom-call.9
  480.8 9.8 custom-call.10
  490.6 52.6 %all-reduce.14.cloned.1.call-done = f32[128,128]{1,0:T(8,128)} async-done(((f32[128,128]{1,0:T(8,128)}), f32[128,128]{1,0:T(8,128)}) %all-reduce.14.cloned.1.call-update) | async-done | bytes 65552 | tf_op jit(solution)/shard_map/psum | solution.py:126
  546.6 14.6 %fusion = f32[640,128]{1,0:T(8,128)} fusion(f32[2560,128]{1,0:T(8,128)S(1)} %bitcast.133, f32[320,8,5,128]{3,2,1,0:T(8,128)} %bitcast.125), kind=kOutput, calls=%fused_computation | convolution fusion | flops 2516582400 | bytes 8192000 | tf_op jit(solution)/shard_map/nm,nk->mk/dot_general | solution.py:86
  561.3 65.7 %all-reduce.22.cloned.1.call-done = (f32[640,128]{1,0:T(8,128)}, f32[5,128,128]{2,1,0:T(8,128)}) async-done(((f32[640,128]{1,0:T(8,128)}, f32[5,128,128]{2,1,0:T(8,128)}), (f32[640,128]{1,0:T(8,128)}, f32[5,128,128]{2,1,0:T(8,128)})) %all-reduce.22.cloned.1.call-update) | async-done | bytes 655376 | tf_op jit(solution)/shard_map/psum | solution.py:18
  628.5 6.1 collective-permute-done.10
  638.5 10.9 %collective-permute-done.11 = f32[5,128,128]{2,1,0:T(8,128)S(1)} collective-permute-done((f32[5,128,128]{2,1,0:T(8,128)S(1)}, f32[5,128,128]{2,1,0:T(8,128)S(1)}, u32[]{:S(2)}, u32[]{:S(2)}) %collective-permute-start.11) | collective-permute-done | bytes 327712 | tf_op jit(solution)/shard_map/ppermute | solution.py:13
  655.2 10.1 %fusion.2 = f32[2560,128]{1,0:T(8,128)} fusion(f32[640,128]{1,0:T(8,128)S(1)} %copy-done.4, f32[320,8,5,128]{3,2,1,0:T(8,128)} %bitcast.126), kind=kOutput, calls=%fused_computation.2 | convolution fusion | flops 2516582400 | bytes 8192000 | tf_op jit(solution)/shard_map/dot_general | solution.py:80
  669.8 6.5 collective-permute-done.13
  680.6 14.4 %collective-permute-done.14 = f32[5,2,128,128]{3,2,0,1:T(8,128)S(1)} collective-permute-done((f32[5,2,128,128]{3,2,0,1:T(8,128)S(1)}, f32[5,2,128,128]{3,2,0,1:T(8,128)S(1)}, u32[]{:S(2)}, u32[]{:S(2)}) %collective-permute-start.14) | collective-permute-done | bytes 655392 | tf_op jit(solution)/shard_map/ppermute | solution.py:13
  696.3 126.0 %all-reduce.16.cloned.1.call-done = f32[2560,128]{1,0:T(8,128)} async-done(((f32[2560,128]{1,0:T(8,128)}), f32[2560,128]{1,0:T(8,128)}) %all-reduce.16.cloned.1.call-update) | async-done | bytes 1310736 | tf_op jit(solution)/shard_map/psum | solution.py:101
  830.5 59.3 %all-reduce.18.cloned.1.call-done = f32[128,128]{0,1:T(8,128)} async-done(((f32[128,128]{0,1:T(8,128)}), f32[128,128]{0,1:T(8,128)}) %all-reduce.18.cloned.1.call-update) | async-done | bytes 65552 | tf_op jit(solution)/shard_map/psum | solution.py:126
  891.6 11.7 %cholesky.81 = f32[128,128]{1,0:T(8,128)S(1)} custom-call(f32[128,128]{1,0:T(8,128)S(1)} %fusion.18), custom_call_target="Cholesky" | custom-call | tf_op jit(solution)/shard_map/jit(cholesky)/cholesky | solution.py:43
  904.7 9.8 custom-call.11
  920.9 65.6 %all-reduce.20.cloned.1.call-done = f32[2,5,128,128]{3,2,1,0:T(8,128)} async-done(((f32[2,5,128,128]{3,2,1,0:T(8,128)}), f32[2,5,128,128]{3,2,1,0:T(8,128)}) %all-reduce.20.cloned.1.call-update) | async-done | bytes 655376 | tf_op jit(solution)/shard_map/psum | solution.py:18
  (103 shorter events, 97.3 us)
Async XLA Ops:
  7.2 164.8 %all-reduce.26.cloned.1.call-start = ((), (), s32[]{:S(2)}) async-start(), calls=%async_computation.7 | async-start | bytes 1310720 | tf_op jit(solution)/shard_map/psum | solution.py:18
  7.2 9.9 collective-permute-start
  18.1 17.4 %collective-permute-start.1 = (f32[5,128,128]{2,1,0:T(8,128)S(1)}, f32[5,128,128]{2,1,0:T(8,128)S(1)}, u32[]{:S(2)}, u32[]{:S(2)}) collective-permute-start(f32[5,128,128]{2,1,0:T(8,128)S(1)} %broadcast_select_fusion.2), channel_id=1, source_target_pairs={{0,2},{1,3},{2,0},{3,1},{4,6},{5,7},{6,4},{7,5},{8,10},{9,11},{10,... | collective-permute-start | bytes 983048 | tf_op jit(solution)/shard_map/ppermute | solution.py:13
  35.6 20.8 %collective-permute-start.2 = (f32[5,128,128]{2,1,0:T(8,128)S(1)}, f32[5,128,128]{2,1,0:T(8,128)S(1)}, u32[]{:S(2)}, u32[]{:S(2)}) collective-permute-start(f32[5,128,128]{2,1,0:T(8,128)S(1)} %broadcast_select_fusion.5), channel_id=1, source_target_pairs={{0,4},{1,5},{2,6},{3,7},{4,0},{5,1},{6,2},{7,3},{8,12},{9,13},{10,... | collective-permute-start | bytes 983048 | tf_op jit(solution)/shard_map/ppermute | solution.py:13
  56.4 7.4 collective-permute-start.3
  63.9 27.2 %collective-permute-start.4 = (f32[5,2,128,128]{3,2,1,0:T(8,128)S(1)}, f32[5,2,128,128]{3,2,1,0:T(8,128)S(1)}, u32[]{:S(2)}, u32[]{:S(2)}) collective-permute-start(f32[5,2,128,128]{3,2,1,0:T(8,128)S(1)} %maximum_select_fusion.3), channel_id=1, source_target_pairs={{0,16},{1,17},{2,18},{3,19},{4,20},{5,21},{6,22},{7,23},{8,24},{9,... | collective-permute-start | bytes 1966088 | tf_op jit(solution)/shard_map/ppermute | solution.py:13
  106.5 260.7 %all-reduce.12.cloned.1.call-start = ((), (), s32[]{:S(2)}) async-start(), calls=%async_computation | async-start | bytes 2621440 | tf_op jit(solution)/shard_map/psum | solution.py:101
  171.9 28.3 %copy-start.5 = (f32[640,128]{1,0:T(8,128)S(1)}, f32[640,128]{1,0:T(8,128)}, u32[]{:S(2)}) copy-start(f32[640,128]{1,0:T(8,128)} %get-tuple-element.8) | copy-start | bytes 983044
  171.9 7.6 collective-permute-start.5
  180.6 13.8 %collective-permute-start.6 = (f32[5,128,128]{2,1,0:T(8,128)S(1)}, f32[5,128,128]{2,1,0:T(8,128)S(1)}, u32[]{:S(2)}, u32[]{:S(2)}) collective-permute-start(f32[5,128,128]{2,1,0:T(8,128)S(1)} %broadcast_select_fusion.1), channel_id=1, source_target_pairs={{0,2},{1,3},{2,0},{3,1},{4,6},{5,7},{6,4},{7,5},{8,10},{9,11},{10,... | collective-permute-start | bytes 983048 | tf_op jit(solution)/shard_map/ppermute | solution.py:13
  194.4 19.7 %collective-permute-start.7 = (f32[5,128,128]{2,1,0:T(8,128)S(1)}, f32[5,128,128]{2,1,0:T(8,128)S(1)}, u32[]{:S(2)}, u32[]{:S(2)}) collective-permute-start(f32[5,128,128]{2,1,0:T(8,128)S(1)} %broadcast_select_fusion.4), channel_id=1, source_target_pairs={{0,4},{1,5},{2,6},{3,7},{4,0},{5,1},{6,2},{7,3},{8,12},{9,13},{10,... | collective-permute-start | bytes 983048 | tf_op jit(solution)/shard_map/ppermute | solution.py:13
  210.4 224.8 %all-reduce.24.cloned.1.call-start = ((), (), s32[]{:S(2)}) async-start(), calls=%async_computation.6 | async-start | bytes 262144 | tf_op jit(solution)/shard_map/psum | solution.py:126
  214.2 7.2 collective-permute-start.8
  221.4 18.6 %collective-permute-start.9 = (f32[5,2,128,128]{3,2,0,1:T(8,128)S(1)}, f32[5,2,128,128]{3,2,0,1:T(8,128)S(1)}, u32[]{:S(2)}, u32[]{:S(2)}) collective-permute-start(f32[5,2,128,128]{3,2,0,1:T(8,128)S(1)} %maximum_select_fusion.4), channel_id=1, source_target_pairs={{0,16},{1,17},{2,18},{3,19},{4,20},{5,21},{6,22},{7,23},{8,24},{9,... | collective-permute-start | bytes 1966088 | tf_op jit(solution)/shard_map/ppermute | solution.py:13
  369.1 2.9 copy-start.2
  372.0 171.2 %all-reduce.14.cloned.1.call-start = ((), (), s32[]{:S(2)}) async-start(), calls=%async_computation.1 | async-start | bytes 131072 | tf_op jit(solution)/shard_map/psum | solution.py:126
  480.1 146.9 %all-reduce.22.cloned.1.call-start = ((), (), s32[]{:S(2)}) async-start(), calls=%async_computation.5 | async-start | bytes 1310720 | tf_op jit(solution)/shard_map/psum | solution.py:18
  545.8 15.4 %copy-start = (f32[20,128,128]{2,1,0:T(8,128)}, f32[20,128,128]{2,1,0:T(8,128)S(1)}, u32[]{:S(2)}) copy-start(f32[20,128,128]{2,1,0:T(8,128)S(1)} %convolution_add_fusion) | copy-start | bytes 3932164
  561.2 261.0 %all-reduce.16.cloned.1.call-start = ((), (), s32[]{:S(2)}) async-start(), calls=%async_computation.2 | async-start | bytes 2621440 | tf_op jit(solution)/shard_map/psum | solution.py:101
  627.0 28.3 %copy-start.4 = (f32[640,128]{1,0:T(8,128)S(1)}, f32[640,128]{1,0:T(8,128)}, u32[]{:S(2)}) copy-start(f32[640,128]{1,0:T(8,128)} %get-tuple-element.4) | copy-start | bytes 983044
  627.0 7.6 collective-permute-start.10
  635.6 13.8 %collective-permute-start.11 = (f32[5,128,128]{2,1,0:T(8,128)S(1)}, f32[5,128,128]{2,1,0:T(8,128)S(1)}, u32[]{:S(2)}, u32[]{:S(2)}) collective-permute-start(f32[5,128,128]{2,1,0:T(8,128)S(1)} %broadcast_select_fusion), channel_id=1, source_target_pairs={{0,2},{1,3},{2,0},{3,1},{4,6},{5,7},{6,4},{7,5},{8,10},{9,11},{10,... | collective-permute-start | bytes 983048 | tf_op jit(solution)/shard_map/ppermute | solution.py:13
  649.4 19.7 %collective-permute-start.12 = (f32[5,128,128]{2,1,0:T(8,128)S(1)}, f32[5,128,128]{2,1,0:T(8,128)S(1)}, u32[]{:S(2)}, u32[]{:S(2)}) collective-permute-start(f32[5,128,128]{2,1,0:T(8,128)S(1)} %broadcast_select_fusion.3), channel_id=1, source_target_pairs={{0,4},{1,5},{2,6},{3,7},{4,0},{5,1},{6,2},{7,3},{8,12},{9,13},{10,... | collective-permute-start | bytes 983048 | tf_op jit(solution)/shard_map/ppermute | solution.py:13
  665.4 224.4 %all-reduce.18.cloned.1.call-start = ((), (), s32[]{:S(2)}) async-start(), calls=%async_computation.3 | async-start | bytes 131072 | tf_op jit(solution)/shard_map/psum | solution.py:126
  669.2 7.2 collective-permute-start.13
  676.4 18.6 %collective-permute-start.14 = (f32[5,2,128,128]{3,2,0,1:T(8,128)S(1)}, f32[5,2,128,128]{3,2,0,1:T(8,128)S(1)}, u32[]{:S(2)}, u32[]{:S(2)}) collective-permute-start(f32[5,2,128,128]{3,2,0,1:T(8,128)S(1)} %maximum_select_fusion.5), channel_id=1, source_target_pairs={{0,16},{1,17},{2,18},{3,19},{4,20},{5,21},{6,22},{7,23},{8,24},{9,... | collective-permute-start | bytes 1966088 | tf_op jit(solution)/shard_map/ppermute | solution.py:13
  822.2 2.1 copy-start.1
  827.3 87.2 %copy-start.6 = (f32[128,128]{1,0:T(8,128)S(1)}, f32[128,128]{1,0:T(8,128)}, u32[]{:S(2)}) copy-start(f32[128,128]{1,0:T(8,128)} %all-reduce.14.cloned.1.call-done) | copy-start | bytes 196612
  827.3 159.2 %all-reduce.20.cloned.1.call-start = ((), (), s32[]{:S(2)}) async-start(), calls=%async_computation.4 | async-start | bytes 1310720 | tf_op jit(solution)/shard_map/psum | solution.py:18
  915.0 2.6 copy-start.3
Sparse Core Ops, SparseCore 0:
  106.6 65.2 all-reduce.25
  210.5 156.6 all-reduce.11
  372.1 63.0 all-reduce.23
  480.2 62.9 all-reduce.13
  561.3 65.5 all-reduce.21
  665.5 156.6 all-reduce.15
  827.4 62.3 all-reduce.17
  921.0 65.3 all-reduce.19
where the time goes:
time: 1000 us; the launch traced here: 996 us
  waiting for transfers between devices  747 us (75%)
  other arithmetic  107 us (11%)
  matrix products  72.8 us (7%)
  starting transfers between devices  46.7 us (5%)
  between operations  14.9 us (1%)
    psum x2, waiting for transfers between devices, rows_whole(): return lax.psum(by_rows, 'col').reshape(shape_out)  252 us
    psum x3, waiting for transfers between devices, spread(): return lax.psum(kept, axis)  197 us
    psum x3, waiting for transfers between devices, reduce_grams(): return lax.psum(stacked, 'row')  175 us
    ppermute x15, waiting for transfers between devices, partner_2(): return lax.ppermute(value, axis, pairs)  124 us
    ppermute x15, starting transfers between devices, partner_2(): return lax.ppermute(value, axis, pairs)  45.8 us
    another operation x9, other arithmetic, solve_spd(): factor = jnp.linalg.cholesky(matrix)  37.2 us
    another operation x6, other arithmetic, solve_spd(): return jax.scipy.linalg.cho_solve((factor, True), target)  31.4 us
    dot_general x2, matrix products, local_products(): jnp.einsum('nm,nk->mk', lower_part, row_set.reshape(-1, columns_n), preci...  29.2 us
  transfers between devices with their start and end apart: 23, of which 22 were waited for; matrix products, arithmetic and copies ran while one was open for 6% of the time, Pallas kernels for 0%

commit v1 on v0

--- a/solution.py
+++ b/solution.py
@@ -123,7 +123,7 @@
     start_set = rhs.reshape(col_blocks, block_size, columns_n)
 
     def reduce_grams(stacked):
-        return lax.psum(stacked, "row")
+        return jnp.sum(lax.all_gather(stacked, "row"), axis=0)
 
     vectors = to_rowset(start_set, row_index, col_index)
     solution = jnp.zeros_like(vectors)

time: 1000 us -> 838 us (0.84)
  waiting for transfers between devices: 747 us -> 538 us
  blocking collectives: 0 us -> 57.4 us
    psum x3 -> x0, waiting for transfers between devices: 175 us -> none  [reduce_grams(): return lax.psum(stacked, 'row')]
    all_gather x0 -> x4, blocking collectives: none -> 57.4 us  [reduce_grams(): return jnp.sum(lax.all_gather(stacked, 'row'), axis=0)]
    ppermute x15, waiting for transfers between devices: 124 us -> 105 us  [partner_2(): return lax.ppermute(value, axis, pairs)]
    psum x2, waiting for transfers between devices: 252 us -> 238 us  [rows_whole(): return lax.psum(by_rows, 'col').reshape(shape_out)]
  transfers between devices with their start and end apart: 23 -> 20, of which waited for: 22 -> 17; matrix products, arithmetic and copies ran while one was open for 6% -> 9% of each run, Pallas kernels for 0% -> 0%
where the time goes in v1:
time: 838 us; the launch traced here: 829 us
  waiting for transfers between devices  538 us (64%)
  other arithmetic  102 us (12%)
  matrix products  68.5 us (8%)
  blocking collectives  57.4 us (7%)
  starting transfers between devices  44.9 us (5%)
  between operations  14.4 us (2%)
    psum x2, waiting for transfers between devices, rows_whole(): return lax.psum(by_rows, 'col').reshape(shape_out)  238 us
    psum x3, waiting for transfers between devices, spread(): return lax.psum(kept, axis)  194 us
    ppermute x15, waiting for transfers between devices, partner_2(): return lax.ppermute(value, axis, pairs)  105 us
    all_gather x4, blocking collectives, reduce_grams(): return jnp.sum(lax.all_gather(stacked, 'row'), axis=0)  57.4 us
    ppermute x15, starting transfers between devices, partner_2(): return lax.ppermute(value, axis, pairs)  44.7 us
    another operation x9, other arithmetic, solve_spd(): factor = jnp.linalg.cholesky(matrix)  37.2 us
    another operation x6, other arithmetic, solve_spd(): return jax.scipy.linalg.cho_solve((factor, True), target)  31.4 us
    dot_general x2, matrix products, local_products(): jnp.einsum('nm,nk->mk', lower_part, row_set.reshape(-1, columns_n), preci...  29.2 us
  transfers between devices with their start and end apart: 20, of which 17 were waited for; matrix products, arithmetic and copies ran while one was open for 9% of the time, Pallas kernels for 0%

profile of v1, /device:TPU:2, one launch (start us, length us, event | category | flops | bytes accessed | tf_op | source)
XLA Modules:
  0.0 829.0 jit_solution(2438360447609790277)
XLA Ops:
  9.2 7.9 collective-permute-done
  21.5 14.1 %collective-permute-done.1 = f32[5,128,128]{2,1,0:T(8,128)S(1)} collective-permute-done((f32[5,128,128]{2,1,0:T(8,128)S(1)}, f32[5,128,128]{2,1,0:T(8,128)S(1)}, u32[]{:S(2)}, u32[]{:S(2)}) %collective-permute-start.1) | collective-permute-done | bytes 327712 | tf_op jit(solution)/shard_map/ppermute | solution.py:13
  35.6 6.3 collective-permute-start.2
  41.9 14.5 %collective-permute-done.2 = f32[5,128,128]{2,1,0:T(8,128)S(1)} collective-permute-done((f32[5,128,128]{2,1,0:T(8,128)S(1)}, f32[5,128,128]{2,1,0:T(8,128)S(1)}, u32[]{:S(2)}, u32[]{:S(2)}) %collective-permute-start.2) | collective-permute-done | bytes 327712 | tf_op jit(solution)/shard_map/ppermute | solution.py:13
  57.1 6.7 collective-permute-done.3
  67.2 23.9 %multiply_reduce_fusion = f32[20,128,5,128]{3,2,1,0:T(8,128)} fusion(f32[20,1,128,5,1,128]{5,4,3,2,1,0:T(1,128)} %param.5, f32[20,5]{1,0:T(8,128)S(1)} %select_select_fusion.3), kind=kLoop, calls=%fused_computation.8 | loop fusion | flops 1638400 | bytes 13107600 | tf_op jit(solution)/shard_map/mul | solution.py:121
  91.9 14.6 %fusion.4 = f32[640,128]{1,0:T(8,128)} fusion(f32[2560,128]{1,0:T(8,128)S(1)} %bitcast.133, f32[320,8,5,128]{3,2,1,0:T(8,128)} %bitcast.129), kind=kOutput, calls=%fused_computation.4 | convolution fusion | flops 2516582400 | bytes 8192000 | tf_op jit(solution)/shard_map/nm,nk->mk/dot_general | solution.py:86
  106.6 65.4 %all-reduce.16.cloned.1.call-done = (f32[640,128]{1,0:T(8,128)}, f32[5,128,128]{2,1,0:T(8,128)}) async-done(((f32[640,128]{1,0:T(8,128)}, f32[5,128,128]{2,1,0:T(8,128)}), (f32[640,128]{1,0:T(8,128)}, f32[5,128,128]{2,1,0:T(8,128)})) %all-reduce.16.cloned.1.call-update) | async-done | bytes 655376 | tf_op jit(solution)/shard_map/psum | solution.py:18
  173.5 6.1 collective-permute-done.5
  183.7 10.9 %collective-permute-done.6 = f32[5,128,128]{2,1,0:T(8,128)S(1)} collective-permute-done((f32[5,128,128]{2,1,0:T(8,128)S(1)}, f32[5,128,128]{2,1,0:T(8,128)S(1)}, u32[]{:S(2)}, u32[]{:S(2)}) %collective-permute-start.6) | collective-permute-done | bytes 327712 | tf_op jit(solution)/shard_map/ppermute | solution.py:13
  200.5 10.1 %fusion.6 = f32[2560,128]{1,0:T(8,128)} fusion(f32[640,128]{1,0:T(8,128)S(1)} %copy-done.6, f32[320,8,5,128]{3,2,1,0:T(8,128)} %bitcast.130), kind=kOutput, calls=%fused_computation.6 | convolution fusion | flops 2516582400 | bytes 8192000 | tf_op jit(solution)/shard_map/dot_general | solution.py:80
  217.3 16.8 %all-gather.1 = f32[1024,128]{1,0:T(8,128)S(1)} all-gather(f32[128,128]{1,0:T(8,128)S(1)} %convolution_bitcast_fusion.5), channel_id=3, replica_groups=mesh['row'=8,'col'=32] {'row'}, dimensions={0}, use_global_device_ids=true | all-gather | bytes 589824 | tf_op jit(solution)/shard_map/all_gather | solution.py:126
  236.9 11.7 %cholesky.70 = f32[128,128]{1,0:T(8,128)S(1)} custom-call(f32[128,128]{1,0:T(8,128)S(1)} %fusion.22), custom_call_target="Cholesky" | custom-call | tf_op jit(solution)/shard_map/jit(cholesky)/cholesky | solution.py:43
  250.0 9.8 %custom-call.10 = f32[1,128,128]{1,2,0:T(8,128)S(1)} custom-call(f32[1,128,128]{2,1,0:T(8,128)S(1)} %fusion.13), custom_call_target="InvertDiagBlocksLowerTriangular" | custom-call | tf_op jit(solution)/shard_map/jit(_cho_solve)/triangular_solve | solution.py:44
  260.0 110.8 %all-reduce.8.cloned.1.call-done = f32[2560,128]{1,0:T(8,128)} async-done(((f32[2560,128]{1,0:T(8,128)}), f32[2560,128]{1,0:T(8,128)}) %all-reduce.8.cloned.1.call-update) | async-done | bytes 1310736 | tf_op jit(solution)/shard_map/psum | solution.py:101
  374.5 13.7 %all-gather = f32[1024,128]{1,0:T(8,128)S(1)} all-gather(f32[128,128]{1,0:T(8,128)S(1)} %fusion.31), channel_id=2, replica_groups=mesh['row'=8,'col'=32] {'row'}, dimensions={0}, use_global_device_ids=true | all-gather | bytes 589824 | tf_op jit(solution)/shard_map/all_gather | solution.py:126
  388.3 11.7 %cholesky.59 = f32[128,128]{1,0:T(8,128)S(1)} custom-call(f32[128,128]{1,0:T(8,128)S(1)} %fusion.26), custom_call_target="Cholesky" | custom-call | tf_op jit(solution)/shard_map/jit(cholesky)/cholesky | solution.py:43
  401.4 9.8 %custom-call.9 = f32[1,128,128]{1,2,0:T(8,128)S(1)} custom-call(f32[1,128,128]{2,1,0:T(8,128)S(1)} %fusion.12), custom_call_target="InvertDiagBlocksLowerTriangular" | custom-call | tf_op jit(solution)/shard_map/jit(_cho_solve)/triangular_solve | solution.py:44
  416.4 13.4 %all-gather.2 = f32[1024,128]{1,0:T(8,128)S(1)} all-gather(f32[128,128]{1,0:T(8,128)S(1)} %convolution_bitcast_fusion.4), channel_id=4, replica_groups=mesh['row'=8,'col'=32] {'row'}, dimensions={0}, use_global_device_ids=true | all-gather | bytes 589824 | tf_op jit(solution)/shard_map/all_gather | solution.py:126
  432.4 14.6 %fusion = f32[640,128]{1,0:T(8,128)} fusion(f32[2560,128]{1,0:T(8,128)S(1)} %bitcast.139, f32[320,8,5,128]{3,2,1,0:T(8,128)} %bitcast.131), kind=kOutput, calls=%fused_computation | convolution fusion | flops 2516582400 | bytes 8192000 | tf_op jit(solution)/shard_map/nm,nk->mk/dot_general | solution.py:86
  447.0 64.5 %all-reduce.14.cloned.1.call-done = (f32[640,128]{1,0:T(8,128)}, f32[5,128,128]{2,1,0:T(8,128)}) async-done(((f32[640,128]{1,0:T(8,128)}, f32[5,128,128]{2,1,0:T(8,128)}), (f32[640,128]{1,0:T(8,128)}, f32[5,128,128]{2,1,0:T(8,128)})) %all-reduce.14.cloned.1.call-update) | async-done | bytes 655376 | tf_op jit(solution)/shard_map/psum | solution.py:18
  513.1 6.1 collective-permute-done.10
  522.8 10.9 %collective-permute-done.11 = f32[5,128,128]{2,1,0:T(8,128)S(1)} collective-permute-done((f32[5,128,128]{2,1,0:T(8,128)S(1)}, f32[5,128,128]{2,1,0:T(8,128)S(1)}, u32[]{:S(2)}, u32[]{:S(2)}) %collective-permute-start.11) | collective-permute-done | bytes 327712 | tf_op jit(solution)/shard_map/ppermute | solution.py:13
  533.8 6.3 collective-permute-start.12
  540.1 10.1 %fusion.2 = f32[2560,128]{1,0:T(8,128)} fusion(f32[640,128]{1,0:T(8,128)S(1)} %copy-done.5, f32[320,8,5,128]{3,2,1,0:T(8,128)} %bitcast.132), kind=kOutput, calls=%fused_computation.2 | convolution fusion | flops 2516582400 | bytes 8192000 | tf_op jit(solution)/shard_map/dot_general | solution.py:80
  554.8 6.5 collective-permute-done.13
  565.6 14.3 %collective-permute-done.14 = f32[5,2,128,128]{3,2,0,1:T(8,128)S(1)} collective-permute-done((f32[5,2,128,128]{3,2,0,1:T(8,128)S(1)}, f32[5,2,128,128]{3,2,0,1:T(8,128)S(1)}, u32[]{:S(2)}, u32[]{:S(2)}) %collective-permute-start.14) | collective-permute-done | bytes 655392 | tf_op jit(solution)/shard_map/ppermute | solution.py:13
  581.2 126.9 %all-reduce.10.cloned.1.call-done = f32[2560,128]{1,0:T(8,128)} async-done(((f32[2560,128]{1,0:T(8,128)}), f32[2560,128]{1,0:T(8,128)}) %all-reduce.10.cloned.1.call-update) | async-done | bytes 1310736 | tf_op jit(solution)/shard_map/psum | solution.py:101
  712.5 13.6 %all-gather.3 = f32[1024,128]{1,0:T(8,128)S(1)} all-gather(f32[128,128]{1,0:T(8,128)S(1)} %convolution_bitcast_fusion.3), channel_id=5, replica_groups=mesh['row'=8,'col'=32] {'row'}, dimensions={0}, use_global_device_ids=true | all-gather | bytes 589824 | tf_op jit(solution)/shard_map/all_gather | solution.py:126
  726.3 11.7 %cholesky.81 = f32[128,128]{1,0:T(8,128)S(1)} custom-call(f32[128,128]{1,0:T(8,128)S(1)} %fusion.18), custom_call_target="Cholesky" | custom-call | tf_op jit(solution)/shard_map/jit(cholesky)/cholesky | solution.py:43
  739.4 9.8 %custom-call.11 = f32[1,128,128]{1,2,0:T(8,128)S(1)} custom-call(f32[1,128,128]{2,1,0:T(8,128)S(1)} %fusion.14), custom_call_target="InvertDiagBlocksLowerTriangular" | custom-call | tf_op jit(solution)/shard_map/jit(_cho_solve)/triangular_solve | solution.py:44
  755.8 64.5 %all-reduce.12.cloned.1.call-done = f32[2,5,128,128]{3,2,1,0:T(8,128)} async-done(((f32[2,5,128,128]{3,2,1,0:T(8,128)}), f32[2,5,128,128]{3,2,1,0:T(8,128)}) %all-reduce.12.cloned.1.call-update) | async-done | bytes 655376 | tf_op jit(solution)/shard_map/psum | solution.py:18
  (103 shorter events, 76.7 us)
Async XLA Ops:
  7.2 164.8 %all-reduce.16.cloned.1.call-start = ((), (), s32[]{:S(2)}) async-start(), calls=%async_computation.4 | async-start | bytes 1310720 | tf_op jit(solution)/shard_map/psum | solution.py:18
  7.2 9.9 %collective-permute-start = (f32[5,128,128]{2,1,0:T(8,128)}, f32[5,128,128]{2,1,0:T(8,128)S(1)}, u32[]{:S(2)}, u32[]{:S(2)}) collective-permute-start(f32[5,128,128]{2,1,0:T(8,128)} %bitcast.153), channel_id=1, source_target_pairs={{0,1},{1,0},{2,3},{3,2},{4,5},{5,4},{6,7},{7,6},{8,9},{9,8},{10,11... | collective-permute-start | bytes 983048 | tf_op jit(solution)/shard_map/ppermute | solution.py:13
  18.1 17.4 %collective-permute-start.1 = (f32[5,128,128]{2,1,0:T(8,128)S(1)}, f32[5,128,128]{2,1,0:T(8,128)S(1)}, u32[]{:S(2)}, u32[]{:S(2)}) collective-permute-start(f32[5,128,128]{2,1,0:T(8,128)S(1)} %broadcast_select_fusion.2), channel_id=1, source_target_pairs={{0,2},{1,3},{2,0},{3,1},{4,6},{5,7},{6,4},{7,5},{8,10},{9,11},{10,... | collective-permute-start | bytes 983048 | tf_op jit(solution)/shard_map/ppermute | solution.py:13
  35.6 20.8 %collective-permute-start.2 = (f32[5,128,128]{2,1,0:T(8,128)S(1)}, f32[5,128,128]{2,1,0:T(8,128)S(1)}, u32[]{:S(2)}, u32[]{:S(2)}) collective-permute-start(f32[5,128,128]{2,1,0:T(8,128)S(1)} %broadcast_select_fusion.5), channel_id=1, source_target_pairs={{0,4},{1,5},{2,6},{3,7},{4,0},{5,1},{6,2},{7,3},{8,12},{9,13},{10,... | collective-permute-start | bytes 983048 | tf_op jit(solution)/shard_map/ppermute | solution.py:13
  56.4 7.4 collective-permute-start.3
  63.9 27.2 %collective-permute-start.4 = (f32[5,2,128,128]{3,2,1,0:T(8,128)S(1)}, f32[5,2,128,128]{3,2,1,0:T(8,128)S(1)}, u32[]{:S(2)}, u32[]{:S(2)}) collective-permute-start(f32[5,2,128,128]{3,2,1,0:T(8,128)S(1)} %maximum_select_fusion.3), channel_id=1, source_target_pairs={{0,16},{1,17},{2,18},{3,19},{4,20},{5,21},{6,22},{7,23},{8,24},{9,... | collective-permute-start | bytes 1966088 | tf_op jit(solution)/shard_map/ppermute | solution.py:13
  106.5 264.3 %all-reduce.8.cloned.1.call-start = ((), (), s32[]{:S(2)}) async-start(), calls=%async_computation | async-start | bytes 2621440 | tf_op jit(solution)/shard_map/psum | solution.py:101
  172.0 28.6 %copy-start.6 = (f32[640,128]{1,0:T(8,128)S(1)}, f32[640,128]{1,0:T(8,128)}, u32[]{:S(2)}) copy-start(f32[640,128]{1,0:T(8,128)} %get-tuple-element.6) | copy-start | bytes 983044
  172.0 7.6 collective-permute-start.5
  180.6 14.0 %collective-permute-start.6 = (f32[5,128,128]{2,1,0:T(8,128)S(1)}, f32[5,128,128]{2,1,0:T(8,128)S(1)}, u32[]{:S(2)}, u32[]{:S(2)}) collective-permute-start(f32[5,128,128]{2,1,0:T(8,128)S(1)} %broadcast_select_fusion.1), channel_id=1, source_target_pairs={{0,2},{1,3},{2,0},{3,1},{4,6},{5,7},{6,4},{7,5},{8,10},{9,11},{10,... | collective-permute-start | bytes 983048 | tf_op jit(solution)/shard_map/ppermute | solution.py:13
  194.7 19.7 %collective-permute-start.7 = (f32[5,128,128]{2,1,0:T(8,128)S(1)}, f32[5,128,128]{2,1,0:T(8,128)S(1)}, u32[]{:S(2)}, u32[]{:S(2)}) collective-permute-start(f32[5,128,128]{2,1,0:T(8,128)S(1)} %broadcast_select_fusion.4), channel_id=1, source_target_pairs={{0,4},{1,5},{2,6},{3,7},{4,0},{5,1},{6,2},{7,3},{8,12},{9,13},{10,... | collective-permute-start | bytes 983048 | tf_op jit(solution)/shard_map/ppermute | solution.py:13
  210.7 300.9 %all-reduce.14.cloned.1.call-start = ((), (), s32[]{:S(2)}) async-start(), calls=%async_computation.3 | async-start | bytes 1310720 | tf_op jit(solution)/shard_map/psum | solution.py:18
  214.4 19.8 %collective-permute-start.8 = (f32[5,1,128,128]{3,2,0,1:T(8,128)S(1)}, f32[5,1,128,128]{3,2,0,1:T(8,128)S(1)}, u32[]{:S(2)}, u32[]{:S(2)}) collective-permute-start(f32[5,1,128,128]{3,2,0,1:T(8,128)S(1)} %select_bitcast_fusion.1), channel_id=1, source_target_pairs={{0,8},{1,9},{2,10},{3,11},{4,12},{5,13},{6,14},{7,15},{8,0},{9,1},... | collective-permute-start | bytes 983048 | tf_op jit(solution)/shard_map/ppermute | solution.py:13
  234.3 25.5 %collective-permute-start.9 = (f32[5,2,128,128]{3,2,0,1:T(8,128)S(1)}, f32[5,2,128,128]{3,2,0,1:T(8,128)S(1)}, u32[]{:S(2)}, u32[]{:S(2)}) collective-permute-start(f32[5,2,128,128]{3,2,0,1:T(8,128)S(1)} %maximum_select_fusion.4), channel_id=1, source_target_pairs={{0,16},{1,17},{2,18},{3,19},{4,20},{5,21},{6,22},{7,23},{8,24},{9,... | collective-permute-start | bytes 1966088 | tf_op jit(solution)/shard_map/ppermute | solution.py:13
  372.2 2.3 copy-start.2
  431.5 15.4 %copy-start = (f32[20,128,128]{2,1,0:T(8,128)}, f32[20,128,128]{2,1,0:T(8,128)S(1)}, u32[]{:S(2)}) copy-start(f32[20,128,128]{2,1,0:T(8,128)S(1)} %convolution_add_fusion) | copy-start | bytes 3932164
  447.0 261.2 %all-reduce.10.cloned.1.call-start = ((), (), s32[]{:S(2)}) async-start(), calls=%async_computation.1 | async-start | bytes 2621440 | tf_op jit(solution)/shard_map/psum | solution.py:101
  511.6 28.5 %copy-start.5 = (f32[640,128]{1,0:T(8,128)S(1)}, f32[640,128]{1,0:T(8,128)}, u32[]{:S(2)}) copy-start(f32[640,128]{1,0:T(8,128)} %get-tuple-element.4) | copy-start | bytes 983044
  511.6 7.6 collective-permute-start.10
  520.2 13.6 %collective-permute-start.11 = (f32[5,128,128]{2,1,0:T(8,128)S(1)}, f32[5,128,128]{2,1,0:T(8,128)S(1)}, u32[]{:S(2)}, u32[]{:S(2)}) collective-permute-start(f32[5,128,128]{2,1,0:T(8,128)S(1)} %broadcast_select_fusion), channel_id=1, source_target_pairs={{0,2},{1,3},{2,0},{3,1},{4,6},{5,7},{6,4},{7,5},{8,10},{9,11},{10,... | collective-permute-start | bytes 983048 | tf_op jit(solution)/shard_map/ppermute | solution.py:13
  533.8 20.3 %collective-permute-start.12 = (f32[5,128,128]{2,1,0:T(8,128)S(1)}, f32[5,128,128]{2,1,0:T(8,128)}, u32[]{:S(2)}, u32[]{:S(2)}) collective-permute-start(f32[5,128,128]{2,1,0:T(8,128)S(1)} %broadcast_select_fusion.3), channel_id=1, source_target_pairs={{0,4},{1,5},{2,6},{3,7},{4,0},{5,1},{6,2},{7,3},{8,12},{9,13},{10,... | collective-permute-start | bytes 983048 | tf_op jit(solution)/shard_map/ppermute | solution.py:13
  550.3 270.0 %all-reduce.12.cloned.1.call-start = ((), (), s32[]{:S(2)}) async-start(), calls=%async_computation.2 | async-start | bytes 1310720 | tf_op jit(solution)/shard_map/psum | solution.py:18
  554.1 7.2 collective-permute-start.13
  561.3 18.6 %collective-permute-start.14 = (f32[5,2,128,128]{3,2,0,1:T(8,128)S(1)}, f32[5,2,128,128]{3,2,0,1:T(8,128)S(1)}, u32[]{:S(2)}, u32[]{:S(2)}) collective-permute-start(f32[5,2,128,128]{3,2,0,1:T(8,128)S(1)} %maximum_select_fusion.5), channel_id=1, source_target_pairs={{0,16},{1,17},{2,18},{3,19},{4,20},{5,21},{6,22},{7,23},{8,24},{9,... | collective-permute-start | bytes 1966088 | tf_op jit(solution)/shard_map/ppermute | solution.py:13
  708.1 2.1 copy-start.1
  749.7 2.7 copy-start.3
  749.7 2.7 copy-start.4
Sparse Core Ops, SparseCore 0:
  106.6 65.2 all-reduce.15
  210.8 159.9 all-reduce.7
  447.1 64.3 all-reduce.13
  550.4 157.7 all-reduce.9
  756.0 64.2 all-reduce.11
